TPU v7x, 256 devices: a whole 4x4x8 slice. The times are simulated.
256 devices in a mesh: group: 4 (over z_hi), dp: 8 (over y, z_lo), mp: 8 (over x, core).
Axes of the slice: x: 4, y: 4, z: 8 (z_hi: 4, z_lo: 2; z = z_hi * 2 + z_lo), core: 2. Of those that a mesh axis runs over, the one named last changes fastest.
Arguments:
- inner_columns: float32 [4, 576, 4032], P('group', None, 'mp'), may hold values from -6 to 6
- inner_rows: float32 [4, 2112, 576], P('group', 'mp'), may hold values from -6 to 6
- inner_norms: float32 [4, 3, 576], P('group'), may hold values from -6 to 6
- inner_embed: float32 [4, 8192, 576], P('group', 'mp'), may hold values from -6 to 6
- basis: float32 [576, 64], replicated, may hold values from -0.25 to 0.25
- outer_layer: float32 [8, 442368], P('mp', ('group', 'dp')), may hold values from -6 to 6
- outer_norms: float32 [1728], P(('group', 'dp')), may hold values from -6 to 6
- outer_embed: float32 [8, 1024, 576], P('mp', ('group', 'dp')), may hold values from -6 to 6
- layer_momentum: float32 [8, 442368], P('mp', ('group', 'dp')), may hold values from -6 to 6
- norm_momentum: float32 [1728], P(('group', 'dp')), may hold values from -6 to 6
- embed_momentum: float32 [8, 1024, 576], P('mp', ('group', 'dp')), may hold values from -6 to 6
Outputs:
- new_columns: float32 [576, 4032], P(None, 'mp')
- new_rows: float32 [2112, 576], P('mp')
- new_norms: float32 [3, 576], replicated
- new_embed: float32 [8192, 576], P('mp')
- new_layer_momentum: float32 [8, 442368], P('mp', ('group', 'dp'))
- new_norm_momentum: float32 [1728], P(('group', 'dp'))
- new_embed_momentum: float32 [8, 1024, 576], P('mp', ('group', 'dp'))
All inputs are finite; a program needn't handle non-finite values.
Results may differ from a plain program's by a relative error of at most 0.000076.
Values sent between devices are 32-bit elements; how exact they have to be, the bound alone decides.
No kernel may reach another device: no remote copies, remote signals or barrier semaphores. Data moves between devices by JAX's collectives and lax.ppermute only.
A program may use at most 64 MiB of HBM per device.

v0:
```python
import jax
import jax.numpy as jnp
from jax import lax
from jax.sharding import PartitionSpec as P

MU = 0.5
RATE = 0.7


def nesterov(weights, delta, momentum):
    fresh = MU * momentum + delta
    return (weights - RATE * (delta + MU * fresh), fresh)


def local(
    inner_columns,
    inner_rows,
    inner_norms,
    inner_embed,
    basis,
    outer_layer,
    outer_norms,
    outer_embed,
    layer_momentum,
    norm_momentum,
    embed_momentum,
):
    groups = lax.axis_size("group")
    copies = lax.axis_size("dp")
    place = lax.axis_index("dp")
    width = inner_columns.shape[1]
    col_width = inner_columns.shape[2]

    def own_pieces(flat):
        table = flat.reshape(groups, copies, -1)
        return lax.dynamic_index_in_dim(table, place, 1, keepdims=False)

    layer_pieces = own_pieces(
        jnp.concatenate([inner_columns[0].reshape(-1), inner_rows[0].reshape(-1)])
    )
    norm_pieces = own_pieces(inner_norms[0].reshape(-1))
    embed_rows = inner_embed[0]
    row_table = embed_rows.reshape(groups, copies, -1, width)
    row_pieces = lax.dynamic_index_in_dim(row_table, place, 1, keepdims=False)
    outer_rows = outer_embed[0]
    layer_sum, norm_sum, rows_sum = (
        lax.psum_scatter(layer_pieces, "group", scatter_dimension=0, tiled=True),
        lax.psum_scatter(norm_pieces, "group", scatter_dimension=0, tiled=True),
        lax.psum_scatter(row_pieces, "group", scatter_dimension=0, tiled=True),
    )
    factor = jnp.dot(
        outer_rows - rows_sum[0] / groups,
        basis,
        precision=lax.Precision.HIGHEST,
        preferred_element_type=jnp.float32,
    )
    embed_delta = jnp.dot(
        factor, basis.T, precision=lax.Precision.HIGHEST, preferred_element_type=jnp.float32
    )
    outer_piece = outer_layer[0]
    new_layer, new_layer_m = nesterov(
        outer_piece, outer_piece - layer_sum[0] / groups, layer_momentum[0]
    )
    new_norm, new_norm_m = nesterov(outer_norms, outer_norms - norm_sum[0] / groups, norm_momentum)
    new_embed_rows, new_embed_m = nesterov(outer_rows, embed_delta, embed_momentum[0])
    pieces = (new_layer[None, :], new_norm[None, :], new_embed_rows)
    layer_all, norm_all, embed_all = (
        lax.all_gather(pieces[0], ("group", "dp"), axis=0, tiled=True),
        lax.all_gather(pieces[1], ("group", "dp"), axis=0, tiled=True),
        lax.all_gather(pieces[2], ("group", "dp"), axis=0, tiled=True),
    )
    layer_whole = layer_all.reshape(-1)
    split = width * col_width
    new_columns = layer_whole[:split].reshape(width, col_width)
    new_rows = layer_whole[split:].reshape(-1, width)
    new_norms = norm_all.reshape(3, width)
    return (
        new_columns,
        new_rows,
        new_norms,
        embed_all,
        new_layer_m[None, :],
        new_norm_m,
        new_embed_m[None, :, :],
    )


def solution(mesh):
    in_specs = (
        P("group", None, "mp"),
        P("group", "mp", None),
        P("group", None, None),
        P("group", "mp", None),
        P(),
        P("mp", ("group", "dp")),
        P(("group", "dp")),
        P("mp", ("group", "dp"), None),
        P("mp", ("group", "dp")),
        P(("group", "dp")),
        P("mp", ("group", "dp"), None),
    )
    out_specs = (
        P(None, "mp"),
        P("mp", None),
        P(),
        P("mp", None),
        P("mp", ("group", "dp")),
        P(("group", "dp")),
        P("mp", ("group", "dp"), None),
    )
    return jax.shard_map(local, mesh=mesh, in_specs=in_specs, out_specs=out_specs, check_vma=False)
```

profile of v0, /device:TPU:6, one launch (start us, length us, event | category | flops | bytes accessed | tf_op | source)
XLA Modules:
  0.0 396.3 jit_solution(6770101458662133229)
XLA Ops:
  7.2 2.3 reshape_squeeze.10
  9.6 1.1 reshape_squeeze.9
  10.7 1.2 pad_maximum_fusion
  11.9 1.7 reshape.37
  13.5 1.6 constant_dynamic-slice_fusion.2
  15.2 0.7 copy.28
  16.0 2.1 copy.23
  18.2 0.8 dynamic-slice_bitcast_fusion
  19.7 50.2 %all-reduce.5.cloned.1.call-done = f32[4,13824]{1,0:T(4,128)} async-done(((f32[4,13824]{1,0:T(4,128)}), f32[4,13824]{1,0:T(4,128)}) %all-reduce.5.cloned.1.call-update) | async-done | bytes 221200
  69.9 2.4 subtract_bitcast_fusion
  72.3 25.3 %reduce-scatter.2.cloned.1.call-done = f32[1,32,576]{2,1,0:T(8,128)} async-done(((f32[4,32,576]{2,1,0:T(8,128)}), f32[1,32,576]{2,1,0:T(8,128)}) %reduce-scatter.2.cloned.1.call-update) | async-done | bytes 73744 | tf_op jit(solution)/shard_map/reduce_scatter | solution.py:49
  97.6 1.2 fusion
  98.8 0.9 fusion.3
  101.1 11.7 %all-reduce.2 = f32[4,54]{1,0:T(4,128)S(1)} all-reduce(f32[4,54]{1,0:T(4,128)S(1)} %bitcast.44), channel_id=4, replica_groups=mesh['group'=4,'dp'=8,'mp'=8] {'group'}, use_global_device_ids=true, to_apply=%region_1.2.clone | all-reduce | flops 216 | bytes 1728
  112.8 1.2 subtract_dynamic-update-slice_fusion
  114.0 73.0 %all-reduce = f32[1728]{0:T(1024)S(1)} all-reduce(f32[1728]{0:T(1024)S(1)} %get-tuple-element.28), channel_id=2, replica_groups=mesh['group'=4,'dp'=8,'mp'=8] {'group','dp'}, use_global_device_ids=true, to_apply=%add | all-reduce | flops 1728 | bytes 13824
  187.0 0.7 reshape.40
  187.7 54.7 %all-gather.7.cloned.1.call-done = f32[32,1,13824]{2,1,0:T(1,128)} async-done(((f32[1,1,13824]{2,1,0:T(1,128)}), f32[32,1,13824]{2,1,0:T(1,128)}) %all-gather.7.cloned.1.call-update) | async-done | bytes 1769488 | tf_op jit(solution)/shard_map/all_gather | solution.py:68
  242.4 2.8 slice_reduce_fusion.1
  245.1 1.1 reshape.39
  246.2 3.0 slice_reduce_fusion
  249.2 2.4 reshape.38
  251.5 135.1 %all-gather.5.cloned.1.call-done = f32[1024,576]{1,0:T(8,128)} async-done(((f32[32,576]{1,0:T(8,128)}), f32[1024,576]{1,0:T(8,128)}) %all-gather.5.cloned.1.call-update) | async-done | bytes 2359312 | tf_op jit(solution)/shard_map/all_gather | solution.py:70
  386.7 3.1 copy.24
  (38 shorter events, 1.6 us)
Async XLA Ops:
  7.2 90.4 %copy-start = (f32[576,64]{0,1:T(8,128)S(1)}, f32[576,64]{0,1:T(8,128)}, u32[]{:S(2)}) copy-start(f32[576,64]{0,1:T(8,128)} %param.15) | copy-start | bytes 442372
  7.2 2.4 copy-start.2
  7.2 62.7 %all-reduce.5.cloned.1.call-start = ((), (), s32[]{:S(2)}) async-start(), calls=%async_computation.4 | async-start | bytes 442368
  15.9 3.1 copy-start.11
  15.9 53.9 %copy-start.5 = (f32[1,13824]{1,0:T(1,128)S(1)}, f32[1,13824]{1,0:T(1,128)}, u32[]{:S(2)}) copy-start(f32[1,13824]{1,0:T(1,128)} %param.16) | copy-start | bytes 165892
  16.0 53.9 %copy-start.6 = (f32[1,13824]{1,0:T(1,128)S(1)}, f32[1,13824]{1,0:T(1,128)}, u32[]{:S(2)}) copy-start(f32[1,13824]{1,0:T(1,128)} %param.19) | copy-start | bytes 165892
  16.0 81.6 %copy-start.3 = (f32[1,32,576]{2,1,0:T(8,128)S(1)}, f32[1,32,576]{2,1,0:T(8,128)}, u32[]{:S(2)}) copy-start(f32[1,32,576]{2,1,0:T(8,128)} %param.18) | copy-start | bytes 221188
  16.0 82.8 %copy-start.4 = (f32[1,32,576]{2,1,0:T(8,128)S(1)}, f32[1,32,576]{2,1,0:T(8,128)}, u32[]{:S(2)}) copy-start(f32[1,32,576]{2,1,0:T(8,128)} %param.21) | copy-start | bytes 221188
  16.0 81.6 %reduce-scatter.2.cloned.1.call-start = ((), (), s32[]{:S(2)}) async-start(), calls=%async_computation.1 | async-start | bytes 409600 | tf_op jit(solution)/shard_map/reduce_scatter | solution.py:49
  18.2 81.5 %copy-start.7 = (f32[1,3,576]{2,0,1:T(1,128)S(1)}, f32[1,3,576]{2,0,1:T(1,128)}, u32[]{:S(2)}) copy-start(f32[1,3,576]{2,0,1:T(1,128)} %param.13) | copy-start | bytes 20740
  18.2 81.6 %copy-start.10 = (u32[256]{0:T(256)S(1)}, u32[256]{0:T(256)}, u32[]{:S(2)}) copy-start(u32[256]{0:T(256)} %constant.46) | copy-start | bytes 3076
  18.2 94.5 %copy-start.8 = (f32[54]{0:T(128)S(1)}, f32[54]{0:T(128)}, u32[]{:S(2)}) copy-start(f32[54]{0:T(128)} %param.17) | copy-start | bytes 652
  18.2 94.5 %copy-start.9 = (f32[54]{0:T(128)S(1)}, f32[54]{0:T(128)}, u32[]{:S(2)}) copy-start(f32[54]{0:T(128)} %param.20) | copy-start | bytes 652
  19.0 223.3 %all-gather.7.cloned.1.call-start = ((), (), s32[]{:S(2)}) async-start(), calls=%async_computation.3 | async-start | bytes 1824768 | tf_op jit(solution)/shard_map/all_gather | solution.py:68
  72.3 314.4 %all-gather.5.cloned.1.call-start = ((), (), s32[]{:S(2)}) async-start(), calls=%async_computation.2 | async-start | bytes 2703360 | tf_op jit(solution)/shard_map/all_gather | solution.py:70
  242.4 3.8 copy-start.1
Sparse Core Ops, SparseCore 0:
  16.1 53.7 all-reduce.4
  72.9 24.5 reduce-scatter.1
  99.9 142.3 all-gather.6
  244.6 142.0 all-gather.4
where the time goes:
time: 397 us; the launch traced here: 396 us
  waiting for transfers between devices  265 us (67%)
  blocking collectives  84.7 us (21%)
  local copies, waits for them, and re-layouts  24.7 us (6%)
  between operations  14.6 us (4%)
  other arithmetic  4.81 us (1%)
    all_gather x1, waiting for transfers between devices, local(): lax.all_gather(pieces[2], ('group', 'dp'), axis=0, tiled=True)  135 us
    unnamed x2, blocking collectives  84.7 us
    all_gather x1, waiting for transfers between devices, local(): lax.all_gather(pieces[0], ('group', 'dp'), axis=0, tiled=True)  54.7 us
    unnamed x5, waiting for transfers between devices  50.2 us
    reduce_scatter x1, waiting for transfers between devices, local(): lax.psum_scatter(row_pieces, 'group', scatter_dimension=0, tiled=True)  25.3 us
  transfers between devices with their start and end apart: 4, of which 4 were waited for; matrix products, arithmetic and copies ran while one was open for 5% of the time, Pallas kernels for 0%

commit v1 on v0

--- a/solution.py
+++ b/solution.py
@@ -1,10 +1,22 @@
+import functools
 import jax
 import jax.numpy as jnp
 from jax import lax
 from jax.sharding import PartitionSpec as P
+from jax.lax import all_to_all, axis_size
 
 MU = 0.5
 RATE = 0.7
+
+
+def _read_marks(inputs, comm_axis):
+    current_arr = jnp.concatenate(
+        all_to_all(jnp.stack([inputs] * axis_size(comm_axis)), comm_axis, 0, 0), axis=0
+    )
+    return current_arr
+
+
+proceed_the_terms = functools.partial(_read_marks, comm_axis=("group", "dp"))
 
 
 def nesterov(weights, delta, momentum):
@@ -67,7 +79,7 @@
     layer_all, norm_all, embed_all = (
         lax.all_gather(pieces[0], ("group", "dp"), axis=0, tiled=True),
         lax.all_gather(pieces[1], ("group", "dp"), axis=0, tiled=True),
-        lax.all_gather(pieces[2], ("group", "dp"), axis=0, tiled=True),
+        proceed_the_terms(pieces[2]),
     )
     layer_whole = layer_all.reshape(-1)
     split = width * col_width

time: 397 us -> 271 us (0.68)
  waiting for transfers between devices: 265 us -> 120 us
  starting transfers between devices: 0.16 us -> 7.72 us
  blocking collectives: 84.7 us -> 91.3 us
  local copies, waits for them, and re-layouts: 24.7 us -> 29.8 us
    all_gather x1 -> x0, waiting for transfers between devices: 135 us -> none  [local(): lax.all_gather(pieces[2], ('group', 'dp'), axis=0, tiled=True)]
    all_to_all x0 -> x1, starting transfers between devices: none -> 7.6 us  [_read_marks(): all_to_all(jnp.stack([inputs] * axis_size(comm_axis)), comm_axis, 0, 0)]
    unnamed x2, blocking collectives: 84.7 us -> 91.3 us
    all_gather x1, waiting for transfers between devices: 54.7 us -> 50.5 us  [local(): lax.all_gather(pieces[0], ('group', 'dp'), axis=0, tiled=True)]
    unnamed x5 -> x4, waiting for transfers between devices: 50.2 us -> 47.9 us
  transfers between devices with their start and end apart: 4 -> 4, of which waited for: 4 -> 3; matrix products, arithmetic and copies ran while one was open for 5% -> 12% of each run, Pallas kernels for 0% -> 0%
where the time goes in v1:
time: 271 us; the launch traced here: 270 us
  waiting for transfers between devices  120 us (44%)
  blocking collectives  91.3 us (34%)
  local copies, waits for them, and re-layouts  29.8 us (11%)
  between operations  14.6 us (5%)
  starting transfers between devices  7.72 us (3%)
  other arithmetic  4.81 us (2%)
    unnamed x2, blocking collectives  91.3 us
    all_gather x1, waiting for transfers between devices, local(): lax.all_gather(pieces[0], ('group', 'dp'), axis=0, tiled=True)  50.5 us
    unnamed x4, waiting for transfers between devices  47.9 us
    reduce_scatter x1, waiting for transfers between devices, local(): lax.psum_scatter(row_pieces, 'group', scatter_dimension=0, tiled=True)  21.6 us
    all_to_all x1, starting transfers between devices, _read_marks(): all_to_all(jnp.stack([inputs] * axis_size(comm_axis)), comm_axis, 0, 0)  7.6 us
    unnamed x30, local copies, waits for them, and re-layouts  6.18 us
  transfers between devices with their start and end apart: 4, of which 3 were waited for; matrix products, arithmetic and copies ran while one was open for 12% of the time, Pallas kernels for 0%

profile of v1, /device:TPU:6, one launch (start us, length us, event | category | flops | bytes accessed | tf_op | source)
XLA Modules:
  0.0 270.2 jit_solution(345085248202903525)
XLA Ops:
  7.2 2.2 copy.23
  9.4 0.8 dynamic-slice_bitcast_fusion
  10.3 1.1 reshape_squeeze.10
  11.5 1.1 reshape_squeeze.9
  12.6 1.2 pad_maximum_fusion
  13.8 1.7 reshape.42
  15.5 1.6 constant_dynamic-slice_fusion.2
  17.1 0.7 copy.28
  18.5 21.6 %reduce-scatter.2.cloned.1.call-done = f32[1,32,576]{2,1,0:T(8,128)} async-done(((f32[4,32,576]{2,1,0:T(8,128)}), f32[1,32,576]{2,1,0:T(8,128)}) %reduce-scatter.2.cloned.1.call-update) | async-done | bytes 73744 | tf_op jit(solution)/shard_map/reduce_scatter | solution.py:61
  40.0 1.2 fusion
  41.2 0.9 fusion.3
  42.1 1.8 stack.2
  43.9 7.6 %all-to-all-start = ((f32[32,32,576]{2,1,0:T(8,128)}), f32[32,32,576]{2,1,0:T(8,128)S(1)}, u32[]{:S(2)}, u32[]{:S(2)}) async-start(f32[32,32,576]{2,1,0:T(8,128)} %stack.2), calls=%async_computation.1 | async-start | bytes 5242880 | tf_op jit(solution)/shard_map/all_to_all | solution.py:14
  51.6 47.8 %all-reduce.5.cloned.1.call-done = f32[4,13824]{1,0:T(4,128)} async-done(((f32[4,13824]{1,0:T(4,128)}), f32[4,13824]{1,0:T(4,128)}) %all-reduce.5.cloned.1.call-update) | async-done | bytes 221200
  99.4 2.4 subtract_bitcast_fusion
  103.2 17.9 %all-reduce.2 = f32[4,54]{1,0:T(4,128)S(1)} all-reduce(f32[4,54]{1,0:T(4,128)S(1)} %bitcast.46), channel_id=4, replica_groups=mesh['group'=4,'dp'=8,'mp'=8] {'group'}, use_global_device_ids=true, to_apply=%region_1.2.clone | all-reduce | flops 216 | bytes 1728
  121.1 1.2 subtract_dynamic-update-slice_fusion
  122.3 73.4 %all-reduce = f32[1728]{0:T(1024)S(1)} all-reduce(f32[1728]{0:T(1024)S(1)} %get-tuple-element.21), channel_id=2, replica_groups=mesh['group'=4,'dp'=8,'mp'=8] {'group','dp'}, use_global_device_ids=true, to_apply=%add | all-reduce | flops 1728 | bytes 13824
  196.4 50.5 %all-gather.4.cloned.1.call-done = f32[32,1,13824]{2,1,0:T(1,128)} async-done(((f32[1,1,13824]{2,1,0:T(1,128)}), f32[32,1,13824]{2,1,0:T(1,128)}) %all-gather.4.cloned.1.call-update) | async-done | bytes 1769488 | tf_op jit(solution)/shard_map/all_gather | solution.py:80
  246.9 3.6 %slice_reduce_fusion.1 = f32[11,13824]{1,0:T(8,128)} fusion(f32[32,1,13824]{2,1,0:T(1,128)} %all-gather.4.cloned.1.call-done), kind=kLoop, calls=%fused_computation.2 | loop fusion | bytes 1216512 | tf_op jit(solution)/shard_map/slice | solution.py:87
  250.5 2.2 reshape.44
  252.7 5.3 %slice_reduce_fusion = f32[21,13824]{1,0:T(8,128)} fusion(f32[32,1,13824]{2,1,0:T(1,128)} %all-gather.4.cloned.1.call-done), kind=kLoop, calls=%fused_computation.1 | loop fusion | bytes 2322432 | tf_op jit(solution)/shard_map/slice | solution.py:86
  258.1 3.6 %reshape.43 = f32[576,504]{1,0:T(8,128)} reshape(f32[21,13824]{1,0:T(8,128)} %slice_reduce_fusion) | data formatting | bytes 2322432 | tf_op jit(solution)/shard_map/reshape | solution.py:86
  261.7 2.0 copy.24
  (38 shorter events, 2.3 us)
Async XLA Ops:
  7.2 32.9 %copy-start = (f32[576,64]{0,1:T(8,128)S(1)}, f32[576,64]{0,1:T(8,128)}, u32[]{:S(2)}) copy-start(f32[576,64]{0,1:T(8,128)} %param.15) | copy-start | bytes 442372
  7.2 32.8 %reduce-scatter.2.cloned.1.call-start = ((), (), s32[]{:S(2)}) async-start(), calls=%async_computation.2 | async-start | bytes 409600 | tf_op jit(solution)/shard_map/reduce_scatter | solution.py:61
  7.2 3.0 %copy-start.2 = (f32[1,264,576]{2,1,0:T(8,128)S(1)}, f32[1,264,576]{2,1,0:T(8,128)}, u32[]{:S(2)}) copy-start(f32[1,264,576]{2,1,0:T(8,128)} %param.12) | copy-start | bytes 1824772
  10.2 1.3 copy-start.1
  10.2 89.2 %all-reduce.5.cloned.1.call-start = ((), (), s32[]{:S(2)}) async-start(), calls=%async_computation.4 | async-start | bytes 442368
  13.7 4.1 %copy-start.11 = (u32[256]{0:T(256)S(1)}, u32[256]{0:T(256)}, u32[]{:S(2)}) copy-start(u32[256]{0:T(256)} %constant.52) | copy-start | bytes 3076
  13.8 26.3 %copy-start.3 = (f32[1,32,576]{2,1,0:T(8,128)S(1)}, f32[1,32,576]{2,1,0:T(8,128)}, u32[]{:S(2)}) copy-start(f32[1,32,576]{2,1,0:T(8,128)} %param.18) | copy-start | bytes 221188
  13.8 27.4 %copy-start.4 = (f32[1,32,576]{2,1,0:T(8,128)S(1)}, f32[1,32,576]{2,1,0:T(8,128)}, u32[]{:S(2)}) copy-start(f32[1,32,576]{2,1,0:T(8,128)} %param.21) | copy-start | bytes 221188
  43.9 55.5 %copy-start.5 = (f32[1,13824]{1,0:T(1,128)S(1)}, f32[1,13824]{1,0:T(1,128)}, u32[]{:S(2)}) copy-start(f32[1,13824]{1,0:T(1,128)} %param.16) | copy-start | bytes 165892
  43.9 55.5 %copy-start.6 = (f32[1,13824]{1,0:T(1,128)S(1)}, f32[1,13824]{1,0:T(1,128)}, u32[]{:S(2)}) copy-start(f32[1,13824]{1,0:T(1,128)} %param.19) | copy-start | bytes 165892
  43.9 57.9 %copy-start.7 = (f32[1,3,576]{2,0,1:T(1,128)S(1)}, f32[1,3,576]{2,0,1:T(1,128)}, u32[]{:S(2)}) copy-start(f32[1,3,576]{2,0,1:T(1,128)} %param.13) | copy-start | bytes 20740
  43.9 58.1 %copy-start.10 = (u32[256]{0:T(256)S(1)}, u32[256]{0:T(256)}, u32[]{:S(2)}) copy-start(u32[256]{0:T(256)} %constant.46) | copy-start | bytes 3076
  43.9 77.2 %copy-start.8 = (f32[54]{0:T(128)S(1)}, f32[54]{0:T(128)}, u32[]{:S(2)}) copy-start(f32[54]{0:T(128)} %param.17) | copy-start | bytes 652
  43.9 77.2 %copy-start.9 = (f32[54]{0:T(128)S(1)}, f32[54]{0:T(128)}, u32[]{:S(2)}) copy-start(f32[54]{0:T(128)} %param.20) | copy-start | bytes 652
  43.9 217.8 %all-to-all-start = ((f32[32,32,576]{2,1,0:T(8,128)}), f32[32,32,576]{2,1,0:T(8,128)S(1)}, u32[]{:S(2)}, u32[]{:S(2)}) async-start(f32[32,32,576]{2,1,0:T(8,128)} %stack.2), calls=%async_computation.1 | async-start | bytes 5242880 | tf_op jit(solution)/shard_map/all_to_all | solution.py:14
  51.5 195.4 %all-gather.4.cloned.1.call-start = ((), (), s32[]{:S(2)}) async-start(), calls=%async_computation.3 | async-start | bytes 1824768 | tf_op jit(solution)/shard_map/all_gather | solution.py:80
Sparse Core Ops, SparseCore 0:
  11.1 28.8 reduce-scatter.1
  43.2 56.1 all-reduce.4
  101.9 144.9 all-gather.3
